TPU v7x, 256 devices: a whole 4x4x8 slice. The times are simulated.
256 devices in a mesh: dp: 32 (over x, z), frame: 8 (over y, core).
Axes of the slice: x: 4, y: 4, z: 8, core: 2. Of those that a mesh axis runs over, the one named last changes fastest.
Arguments:
- features: bfloat16 [32, 16, 32, 64, 128], P('dp', 'frame'), may hold values from -6 to 6
- vis_block: int32 [32, 16, 16, 2], P('dp', None, 'frame'), may hold values from 0 to 31
- vis_count: int32 [32, 16, 16], P('dp', None, 'frame'), may hold values from 1 to 2
- query_frame: int32 [32, 256], P('dp'), may hold values from 0 to 15
- query_block: int32 [32, 256], P('dp'), may hold values from 0 to 31
- query_cell: int32 [32, 256], P('dp'), may hold values from 0 to 63
- cotangent: bfloat16 [32, 4, 256, 16], P('dp', None, 'frame')
- w_in: bfloat16 [128, 384], replicated, may hold values from -0.5 to 0.5
- gain: float32 [384], replicated, may hold values from 0.1 to 1.9
- w_qkv: bfloat16 [384, 1152], replicated, may hold values from -0.3125 to 0.3125
- w_out: bfloat16 [384, 384], replicated, may hold values from -0.3125 to 0.3125
- w_head: bfloat16 [4, 384], replicated, may hold values from -0.3125 to 0.3125
Outputs:
- grad_in: float32 [128, 384], replicated
- grad_gain: float32 [384], replicated
- grad_qkv: float32 [384, 1152], replicated
- grad_out: float32 [384, 384], replicated
- grad_head: float32 [4, 384], replicated
Inputs may be any that keep to these rules, and one draw needn't show every extreme that they name: vis_count counts the leading visible slots of vis_block.
All inputs are finite; a program needn't handle non-finite values.
Results may differ from a plain program's by a relative error of at most 0.012.
Values may be sent and summed in bfloat16 or wider, within the bound.
No kernel may reach another device: no remote copies, remote signals or barrier semaphores. Data moves between devices by JAX's collectives and lax.ppermute only.
A program may use at most 64 MiB of HBM per device.

v0:
```python
import jax
import jax.numpy as jnp
from jax import lax
from jax.sharding import PartitionSpec as P

HEADS = 8


def attend(query, keys, values):
    scale = query.shape[-1] ** (-0.5)
    scores = (
        jnp.einsum("nfhd,nghd->nhfg", query.astype(jnp.float32), keys.astype(jnp.float32)) * scale
    )
    probs = jax.nn.softmax(scores, axis=-1).astype(jnp.bfloat16)
    probs = lax.optimization_barrier(probs)
    mixed = jnp.einsum("nhfg,nghd->nfhd", probs.astype(jnp.float32), values.astype(jnp.float32))
    return mixed.astype(jnp.bfloat16)


def inner_rows(left, right):
    return lax.dot_general(
        left, right, (((0,), (0,)), ((), ())), preferred_element_type=jnp.float32
    )


def outer_cols(left, right):
    return lax.dot_general(
        left, right, (((1,), (1,)), ((), ())), preferred_element_type=jnp.float32
    )


def local_grads(corr, cot, w_in, gain, w_qkv, w_out, w_head):
    tracks, frames, width = corr.shape
    total = tracks * frames
    hid = w_in.shape[1]
    head_size = hid // HEADS
    rows = corr.reshape(total, width)
    x_zero = jnp.dot(rows, w_in, preferred_element_type=jnp.float32)
    centred = x_zero - jnp.mean(x_zero, axis=-1, keepdims=True)
    inv_std = lax.rsqrt(jnp.mean(centred * centred, axis=-1, keepdims=True) + 1e-05)
    normed = centred * inv_std
    hidden = (normed * gain).astype(jnp.bfloat16)
    qkv = jnp.dot(hidden, w_qkv, preferred_element_type=jnp.float32).astype(jnp.bfloat16)
    split = qkv.reshape(tracks, frames, 3, HEADS, head_size)
    mixed, backward = jax.vjp(attend, split[:, :, 0], split[:, :, 1], split[:, :, 2])
    mixed = mixed.reshape(total, hid)
    y_out = (x_zero + jnp.dot(mixed, w_out, preferred_element_type=jnp.float32)).astype(
        jnp.bfloat16
    )
    ct_rows = cot.reshape(cot.shape[0], total)
    g_head = jnp.dot(ct_rows, y_out, preferred_element_type=jnp.float32)
    d_y = inner_rows(ct_rows, w_head)
    d_y16 = d_y.astype(jnp.bfloat16)
    g_out = inner_rows(mixed, d_y16)
    d_mixed = outer_cols(d_y16, w_out).astype(jnp.bfloat16)
    d_q, d_k, d_v = backward(d_mixed.reshape(tracks, frames, HEADS, head_size))
    d_qkv = jnp.stack([d_q, d_k, d_v], axis=2).reshape(total, 3 * hid)
    g_qkv = inner_rows(hidden, d_qkv)
    d_hidden = outer_cols(d_qkv, w_qkv)
    g_gain = jnp.sum(d_hidden * normed, axis=0)
    d_norm = d_hidden * gain
    d_x = (
        inv_std
        * (
            d_norm
            - jnp.mean(d_norm, axis=-1, keepdims=True)
            - normed * jnp.mean(d_norm * normed, axis=-1, keepdims=True)
        )
        + d_y
    )
    d_x16 = d_x.astype(jnp.bfloat16)
    g_in = inner_rows(rows, d_x16)
    return (g_in, g_gain, g_qkv, g_out, g_head)


def body(
    features,
    vis_block,
    vis_count,
    query_frame,
    query_block,
    query_cell,
    cotangent,
    w_in,
    gain,
    w_qkv,
    w_out,
    w_head,
):
    feats = features[0]
    fr_dev = feats.shape[0]
    cells = feats.shape[2]
    width = feats.shape[3]
    trk_dev = cotangent.shape[2]
    frame_pos = lax.axis_index("frame")
    frames_q = query_frame[0]
    blocks_q = query_block[0]
    cells_q = query_cell[0]
    local = frames_q - frame_pos * fr_dev
    inside = (local >= 0) & (local < fr_dev)
    picked = feats[jnp.clip(local, 0, fr_dev - 1), blocks_q, cells_q].astype(jnp.float32)
    query = lax.psum_scatter(
        jnp.where(inside[:, None], picked, 0.0).astype(jnp.bfloat16),
        "frame",
        scatter_dimension=0,
        tiled=True,
    )
    groups = vis_block.shape[1]
    slots = vis_block.shape[3]
    frame_ids = jnp.arange(fr_dev, dtype=jnp.int32)[None, :, None]
    patches = feats[frame_ids, vis_block[0]]
    live = jnp.arange(slots, dtype=jnp.int32)[None, None, :] < vis_count[0][:, :, None]
    patches = jnp.where(live[..., None, None], patches, jnp.zeros((), jnp.bfloat16))
    scale = width ** (-0.5)
    outgoing = patches.reshape(groups, fr_dev, slots, cells * width)
    arrived = lax.all_to_all(outgoing, "frame", split_axis=0, concat_axis=1, tiled=True)
    own_groups = arrived.shape[0]
    all_frames = arrived.shape[1]
    arrived = arrived.reshape(own_groups, all_frames, slots, cells, width)
    corr = jnp.einsum(
        "gtc,gfkpc->gtfkp",
        query.reshape(own_groups, -1, width),
        arrived,
        preferred_element_type=jnp.float32,
    )
    corr = (corr * scale).astype(jnp.bfloat16).reshape(trk_dev, all_frames, slots * cells)
    g_in, g_gain, g_qkv, g_out, g_head = local_grads(
        corr, cotangent[0], w_in, gain, w_qkv, w_out, w_head
    )
    s_in, s_gain, s_qkv, s_out, s_head = lax.psum(
        (g_in, g_gain, g_qkv, g_out, g_head), ("dp", "frame")
    )
    return (s_in, s_gain, s_qkv, s_out, s_head)


def solution(mesh):
    in_specs = (
        P("dp", "frame", None, None, None),
        P("dp", None, "frame", None),
        P("dp", None, "frame"),
        P("dp", None),
        P("dp", None),
        P("dp", None),
        P("dp", None, "frame", None),
        P(),
        P(),
        P(),
        P(),
        P(),
    )
    out_specs = (P(), P(), P(), P(), P())
    return jax.shard_map(body, mesh=mesh, in_specs=in_specs, out_specs=out_specs, check_vma=False)
```

profile of v0, /device:TPU:2, one launch (start us, length us, event | category | flops | bytes accessed | tf_op | source)
XLA Modules:
  0.0 383.4 jit_solution(13826835870761128297)
XLA Ops:
  7.2 0.8 fusion.27
  8.1 0.1 reshape.207
  8.2 0.2 copy-done
  8.4 0.8 gather_fusion.1
  9.2 0.3 gather.10
  9.7 1.9 broadcast_select_fusion
  11.7 4.5 %all-to-all-start = ((bf16[16,2,2,8192]{3,2,1,0:T(2,128)(2,1)}), bf16[16,2,2,8192]{3,2,1,0:T(2,128)(2,1)}, u32[]{:S(2)}, u32[]{:S(2)}) async-start(bf16[16,2,2,8192]{3,2,1,0:T(2,128)(2,1)} %broadcast_select_fusion), calls=%async_computation.1 | async-start | bytes 2097152 | tf_op jit(solution)/shard_map/all_to_all | solution.py:116
  16.3 1.9 gather_fusion
  18.2 0.7 select_convert_fusion
  19.2 0.3 fusion.43
  19.6 1.2 copy.40
  20.7 0.4 convolution_convert_fusion.6
  21.1 1.9 reshape.197
  23.0 9.2 %all-to-all-done = bf16[16,2,2,8192]{3,2,1,0:T(2,128)(2,1)} async-done(((bf16[16,2,2,8192]{3,2,1,0:T(2,128)(2,1)}), bf16[16,2,2,8192]{3,2,1,0:T(2,128)(2,1)}, u32[]{:S(2)}, u32[]{:S(2)}) %all-to-all-start) | async-done | bytes 1048608 | tf_op jit(solution)/shard_map/all_to_all | solution.py:116
  32.2 3.4 copy.29
  35.6 2.7 reshape.196
  38.3 18.2 %reduce-scatter.2.cloned.1.call-done = bf16[32,128]{1,0:T(8,128)(2,1)} async-done(((bf16[256,128]{1,0:T(8,128)(2,1)}), bf16[32,128]{1,0:T(8,128)(2,1)}) %reduce-scatter.2.cloned.1.call-update) | async-done | bytes 8208 | tf_op jit(solution)/shard_map/reduce_scatter | solution.py:102
  56.5 2.1 fusion.13
  58.7 0.2 copy.30
  58.9 0.1 reshape_reshape.3
  59.1 0.3 fusion.41
  59.4 0.1 multiply_reduce_fusion.3
  59.5 3.1 convolution_convert_fusion
  62.7 5.3 %reshape.198 = bf16[32,16,3,8,48]{4,3,2,1,0:T(8,128)(2,1)} reshape(bf16[512,1152]{1,0:T(8,128)(2,1)} %convolution_convert_fusion) | data formatting | bytes 2359296 | tf_op jit(solution)/shard_map/reshape | solution.py:44
  67.9 3.7 fusion.40
  71.6 3.8 fusion.42
  75.4 2.3 convolution_convert_fusion.5
  77.8 1.9 fusion.5
  79.8 1.9 fusion.7
  81.7 2.5 fusion.8
  84.2 1.6 fusion.10
  85.9 0.5 fusion.9
  86.4 0.8 pad_maximum_fusion
  87.2 2.5 copy.39
  89.6 5.0 %reshape.199 = bf16[512,1152]{1,0:T(8,128)(2,1)} reshape(bf16[32,16,3,8,48]{4,3,2,1,0:T(8,128)(2,1)} %copy.39) | data formatting | bytes 2359296 | tf_op jit(solution)/shard_map/reshape | solution.py:57
  94.6 3.3 multiply_reduce_fusion.1
  98.0 1.9 fusion.37
  99.9 1.2 copy.41
  101.1 2.0 reshape.200
  103.2 1.2 fusion.22
  104.4 0.2 copy-done.10
  104.6 1.1 fusion.21
  105.8 0.5 fusion.14
  106.3 74.6 %all-reduce = (f32[384]{0:T(512)}, f32[4,384]{1,0:T(4,128)}) all-reduce(f32[384]{0:T(512)S(1)} %get-tuple-element.5, f32[4,384]{1,0:T(4,128)S(1)} %fusion.14), channel_id=1, replica_groups=mesh['dp'=32,'frame'=8] {'dp','frame'}, use_global_device_ids=true, to_apply=%region_10.11 | all-reduce | flops 1920 | bytes 15360 | tf_op jit(solution)/shard_map/psum | solution.py:130
  180.9 190.4 %all-reduce.4.cloned.1.call-done = (f32[128,384]{1,0:T(8,128)}, f32[384,1152]{1,0:T(8,128)}, f32[384,384]{1,0:T(8,128)}) async-done(((f32[128,384]{1,0:T(8,128)}, f32[384,1152]{1,0:T(8,128)}, f32[384,384]{1,0:T(8,128)}), (f32[128,384]{1,0:T(8,128)}, f32[384,1152]{1,0:T(8,128)}, f32[384,384]{1,0:T(8,128)})) %all-reduce.4.cloned.1.call-update) | async-done | bytes 2555920 | tf_op jit(solution)/shard_map/psum | solution.py:130
  371.3 1.7 copy.85
  372.9 2.8 copy.86
  375.7 0.8 copy.87
  (54 shorter events, 0.8 us)
Async XLA Ops:
  7.2 1.2 copy-start
  8.4 1.1 copy-start.17
  9.7 6.5 %copy-start.15 = (s32[1,256]{1,0:T(1,128)S(1)}, s32[1,256]{1,0:T(1,128)}, u32[]{:S(2)}) copy-start(s32[1,256]{1,0:T(1,128)} %param.15) | copy-start | bytes 3076
  9.7 6.5 %copy-start.18 = (s32[1,256]{1,0:T(1,128)S(1)}, s32[1,256]{1,0:T(1,128)}, u32[]{:S(2)}) copy-start(s32[1,256]{1,0:T(1,128)} %param.17) | copy-start | bytes 3076
  9.7 6.5 %copy-start.19 = (s32[1,256]{1,0:T(1,128)S(1)}, s32[1,256]{1,0:T(1,128)}, u32[]{:S(2)}) copy-start(s32[1,256]{1,0:T(1,128)} %param.16) | copy-start | bytes 3076
  9.7 9.3 %copy-start.14 = (bf16[1,4,32,16]{2,3,1,0:T(8,128)(2,1)S(1)}, bf16[1,4,32,16]{2,3,1,0:T(8,128)(2,1)}, u32[]{:S(2)}) copy-start(bf16[1,4,32,16]{2,3,1,0:T(8,128)(2,1)} %param.18) | copy-start | bytes 12292
  9.7 9.5 %copy-start.16 = (bf16[4,384]{1,0:T(4,128)(2,1)S(1)}, bf16[4,384]{1,0:T(4,128)(2,1)}, u32[]{:S(2)}) copy-start(bf16[4,384]{1,0:T(4,128)(2,1)} %param.23) | copy-start | bytes 9220
  11.7 20.5 %all-to-all-start = ((bf16[16,2,2,8192]{3,2,1,0:T(2,128)(2,1)}), bf16[16,2,2,8192]{3,2,1,0:T(2,128)(2,1)}, u32[]{:S(2)}, u32[]{:S(2)}) async-start(bf16[16,2,2,8192]{3,2,1,0:T(2,128)(2,1)} %broadcast_select_fusion), calls=%async_computation.1 | async-start | bytes 2097152 | tf_op jit(solution)/shard_map/all_to_all | solution.py:116
  16.1 4.6 %copy-start.7 = (bf16[384,384]{1,0:T(8,128)(2,1)S(1)}, bf16[384,384]{1,0:T(8,128)(2,1)}, u32[]{:S(2)}) copy-start(bf16[384,384]{1,0:T(8,128)(2,1)} %param.22) | copy-start | bytes 884740
  16.1 40.4 %reduce-scatter.2.cloned.1.call-start = ((), (), s32[]{:S(2)}) async-start(), calls=%async_computation.2 | async-start | bytes 73728 | tf_op jit(solution)/shard_map/reduce_scatter | solution.py:102
  19.0 352.3 %all-reduce.4.cloned.1.call-start = ((), (), s32[]{:S(2)}) async-start(), calls=%async_computation.3 | async-start | bytes 5111808 | tf_op jit(solution)/shard_map/psum | solution.py:130
  35.6 23.4 %copy-start.12 = (bf16[128,384]{1,0:T(8,128)(2,1)S(1)}, bf16[128,384]{1,0:T(8,128)(2,1)}, u32[]{:S(2)}) copy-start(bf16[128,384]{1,0:T(8,128)(2,1)} %param.19) | copy-start | bytes 294916
  38.3 21.2 %copy-start.13 = (f32[384]{0:T(512)S(1)}, f32[384]{0:T(512)}, u32[]{:S(2)}) copy-start(f32[384]{0:T(512)} %param.20) | copy-start | bytes 4612
  75.4 2.4 copy-start.6
  77.8 1.9 copy-start.9
  79.7 1.9 copy-start.8
  81.7 2.5 copy-start.2
  84.2 1.7 copy-start.1
  94.6 3.3 copy-start.3
  98.0 1.9 copy-start.4
  103.2 1.2 copy-start.5
  103.2 1.5 copy-start.10
  371.3 4.5 %copy-start.11 = (f32[384,384]{1,0:T(8,128)S(1)}, f32[384,384]{1,0:T(8,128)}, u32[]{:S(2)}) copy-start(f32[384,384]{1,0:T(8,128)} %get-tuple-element.28) | copy-start | bytes 1769476
Sparse Core Ops, SparseCore 0:
  20.0 36.4 reduce-scatter.1
  105.9 265.3 all-reduce.3
where the time goes:
time: 384 us; the launch traced here: 383 us
  waiting for transfers between devices  218 us (57%)
  blocking collectives  74.6 us (19%)
  local copies, waits for them, and re-layouts  38.5 us (10%)
  matrix products  27.1 us (7%)
  between operations  14.4 us (4%)
  other arithmetic  6.41 us (2%)
  starting transfers between devices  4.55 us (1%)
    psum x1, waiting for transfers between devices, body(): lax.psum((g_in, g_gain, g_qkv, g_out, g_head), ('dp', 'frame'))  190 us
    psum x1, blocking collectives, body(): lax.psum((g_in, g_gain, g_qkv, g_out, g_head), ('dp', 'frame'))  74.6 us
    reduce_scatter x1, waiting for transfers between devices, body(): lax.psum_scatter(jnp.where(inside[:, None], picked, 0.0).astype(jnp.bfloa...  18.2 us
    all_to_all x1, waiting for transfers between devices, body(): lax.all_to_all(outgoing, 'frame', split_axis=0, concat_axis=1, tiled=True)  9.2 us
  transfers between devices with their start and end apart: 3, of which 3 were waited for; matrix products, arithmetic and copies ran while one was open for 3% of the time, Pallas kernels for 0%

commit v1 on v0

--- a/solution.py
+++ b/solution.py
@@ -128,7 +128,7 @@
         corr, cotangent[0], w_in, gain, w_qkv, w_out, w_head
     )
     s_in, s_gain, s_qkv, s_out, s_head = lax.psum(
-        (g_in, g_gain, g_qkv, g_out, g_head), ("dp", "frame")
+        lax.psum((g_in, g_gain, g_qkv, g_out, g_head), "dp"), "frame"
     )
     return (s_in, s_gain, s_qkv, s_out, s_head)
 

time: 384 us -> 362 us (0.943)
  the two profiles are of different devices: /device:TPU:2 before, /device:TPU:1 now
where the time goes in v1:
time: 362 us; the launch traced here: 361 us
  waiting for transfers between devices  176 us (49%)
  blocking collectives  91 us (25%)
  local copies, waits for them, and re-layouts  38.5 us (11%)
  matrix products  27.1 us (7%)
  between operations  14.1 us (4%)
  starting transfers between devices  7.39 us (2%)
  other arithmetic  6.41 us (2%)
    psum x1, waiting for transfers between devices, body(): lax.psum((g_in, g_gain, g_qkv, g_out, g_head), 'dp')  153 us
    psum x1, blocking collectives, body(): lax.psum((g_in, g_gain, g_qkv, g_out, g_head), 'dp')  59.3 us
    psum x1, blocking collectives, body(): lax.psum(lax.psum((g_in, g_gain, g_qkv, g_out, g_head), 'dp'), 'frame')  31.7 us
    reduce_scatter x1, waiting for transfers between devices, body(): lax.psum_scatter(jnp.where(inside[:, None], picked, 0.0).astype(jnp.bfloa...  15.1 us
    all_to_all x1, waiting for transfers between devices, body(): lax.all_to_all(outgoing, 'frame', split_axis=0, concat_axis=1, tiled=True)  8.32 us
    all_to_all x1, starting transfers between devices, body(): lax.all_to_all(outgoing, 'frame', split_axis=0, concat_axis=1, tiled=True)  7.3 us
  transfers between devices with their start and end apart: 4, of which 3 were waited for; matrix products, arithmetic and copies ran while one was open for 4% of the time, Pallas kernels for 0%

profile of v1, /device:TPU:1, one launch (start us, length us, event | category | flops | bytes accessed | tf_op | source)
XLA Modules:
  0.0 360.9 jit_solution(17100170772471553003)
XLA Ops:
  7.2 0.8 fusion.27
  8.2 0.2 copy-done
  8.4 0.8 gather_fusion.1
  9.2 0.3 gather.10
  9.7 1.9 broadcast_select_fusion
  11.7 7.3 %all-to-all-start = ((bf16[16,2,2,8192]{3,2,1,0:T(2,128)(2,1)}), bf16[16,2,2,8192]{3,2,1,0:T(2,128)(2,1)}, u32[]{:S(2)}, u32[]{:S(2)}) async-start(bf16[16,2,2,8192]{3,2,1,0:T(2,128)(2,1)} %broadcast_select_fusion), calls=%async_computation.1 | async-start | bytes 2097152 | tf_op jit(solution)/shard_map/all_to_all | solution.py:116
  19.0 1.9 gather_fusion
  21.0 0.7 select_convert_fusion
  22.0 0.3 fusion.43
  22.3 1.2 copy.40
  23.5 0.4 convolution_convert_fusion.6
  23.9 1.9 reshape.197
  25.8 8.3 %all-to-all-done = bf16[16,2,2,8192]{3,2,1,0:T(2,128)(2,1)} async-done(((bf16[16,2,2,8192]{3,2,1,0:T(2,128)(2,1)}), bf16[16,2,2,8192]{3,2,1,0:T(2,128)(2,1)}, u32[]{:S(2)}, u32[]{:S(2)}) %all-to-all-start) | async-done | bytes 1048608 | tf_op jit(solution)/shard_map/all_to_all | solution.py:116
  34.1 3.4 copy.29
  37.5 2.7 reshape.196
  40.2 15.1 %reduce-scatter.2.cloned.1.call-done = bf16[32,128]{1,0:T(8,128)(2,1)} async-done(((bf16[256,128]{1,0:T(8,128)(2,1)}), bf16[32,128]{1,0:T(8,128)(2,1)}) %reduce-scatter.2.cloned.1.call-update) | async-done | bytes 8208 | tf_op jit(solution)/shard_map/reduce_scatter | solution.py:102
  55.3 2.1 fusion.13
  57.4 0.2 copy.30
  57.6 0.1 reshape_reshape.3
  57.8 0.3 fusion.41
  58.1 0.1 multiply_reduce_fusion.3
  58.3 3.1 convolution_convert_fusion
  61.4 5.3 %reshape.198 = bf16[32,16,3,8,48]{4,3,2,1,0:T(8,128)(2,1)} reshape(bf16[512,1152]{1,0:T(8,128)(2,1)} %convolution_convert_fusion) | data formatting | bytes 2359296 | tf_op jit(solution)/shard_map/reshape | solution.py:44
  66.7 3.7 %fusion.40 = (bf16[32,16,1,8,48]{4,3,2,1,0:T(8,128)(2,1)}, bf16[32,16,1,8,48]{4,3,2,1,0:T(8,128)(2,1)}, bf16[32,16,1,8,48]{4,3,2,1,0:T(8,128)(2,1)}) fusion(bf16[32,16,3,8,48]{4,3,2,1,0:T(8,128)(2,1)} %reshape.198), kind=kLoop, calls=%fused_computation.78 | loop fusion | bytes 2359296 | tf_op jit(solution)/shard_map/slice | solution.py:45
  70.4 3.8 %fusion.42 = (f32[32,8,16]{2,1,0:T(8,128)S(1)}, f32[32,8,16,16]{3,2,1,0:T(8,128)}) fusion(bf16[32,16,1,8,48]{4,3,2,1,0:T(8,128)(2,1)} %get-tuple-element.20, bf16[32,16,1,8,48]{4,3,2,1,0:T(8,128)(2,1)} %get-tuple-element.19), kind=kOutput, calls=%fused_computation.80 | convolution fusion | flops 6488079 | bytes 1064960 | tf_op jit(solution)/shard_map/jvp()/sub | solution.py:14
  74.2 2.3 convolution_convert_fusion.5
  76.6 1.9 fusion.5
  78.5 1.9 fusion.7
  80.4 2.5 fusion.8
  83.0 1.6 fusion.10
  84.6 0.5 fusion.9
  85.1 0.8 pad_maximum_fusion
  85.9 2.5 copy.39
  88.4 5.0 %reshape.199 = bf16[512,1152]{1,0:T(8,128)(2,1)} reshape(bf16[32,16,3,8,48]{4,3,2,1,0:T(8,128)(2,1)} %copy.39) | data formatting | bytes 2359296 | tf_op jit(solution)/shard_map/reshape | solution.py:57
  93.4 3.3 multiply_reduce_fusion.1
  96.7 1.9 fusion.37
  98.6 1.2 copy.41
  99.9 2.0 reshape.200
  101.9 1.2 fusion.22
  103.2 0.2 copy-done.10
  103.4 1.1 fusion.21
  104.6 153.0 %all-reduce.7.cloned.1.call-done = (f32[128,384]{1,0:T(8,128)}, f32[384,1152]{1,0:T(8,128)}, f32[384,384]{1,0:T(8,128)}) async-done(((f32[128,384]{1,0:T(8,128)}, f32[384,1152]{1,0:T(8,128)}, f32[384,384]{1,0:T(8,128)}), (f32[128,384]{1,0:T(8,128)}, f32[384,1152]{1,0:T(8,128)}, f32[384,384]{1,0:T(8,128)})) %all-reduce.7.cloned.1.call-update) | async-done | bytes 2555920 | tf_op jit(solution)/shard_map/psum | solution.py:131
  257.5 0.5 fusion.14
  258.1 59.3 %all-reduce = (f32[384]{0:T(512)S(1)}, f32[4,384]{1,0:T(4,128)S(1)}) all-reduce(f32[384]{0:T(512)S(1)} %get-tuple-element.5, f32[4,384]{1,0:T(4,128)S(1)} %fusion.14), channel_id=1, replica_groups=mesh['dp'=32,'frame'=8] {'dp'}, use_global_device_ids=true, to_apply=%region_11.12 | all-reduce | flops 1920 | bytes 15360 | tf_op jit(solution)/shard_map/psum | solution.py:131
  317.4 31.7 %all-reduce.2 = (f32[384]{0:T(512)}, f32[4,384]{1,0:T(4,128)}) all-reduce(f32[384]{0:T(512)S(1)} %get-tuple-element.8, f32[4,384]{1,0:T(4,128)S(1)} %get-tuple-element.9), channel_id=1, replica_groups=mesh['dp'=32,'frame'=8] {'frame'}, use_global_device_ids=true, to_apply=%region_12.13 | all-reduce | flops 1920 | bytes 15360 | tf_op jit(solution)/shard_map/psum | solution.py:130
  349.1 1.7 copy.88
  350.8 2.8 copy.89
  353.6 0.8 copy.90
  (58 shorter events, 0.9 us)
Async XLA Ops:
  7.2 1.2 copy-start
  8.4 1.1 copy-start.17
  9.7 9.3 %copy-start.15 = (s32[1,256]{1,0:T(1,128)S(1)}, s32[1,256]{1,0:T(1,128)}, u32[]{:S(2)}) copy-start(s32[1,256]{1,0:T(1,128)} %param.15) | copy-start | bytes 3076
  9.7 9.3 %copy-start.18 = (s32[1,256]{1,0:T(1,128)S(1)}, s32[1,256]{1,0:T(1,128)}, u32[]{:S(2)}) copy-start(s32[1,256]{1,0:T(1,128)} %param.17) | copy-start | bytes 3076
  9.7 9.3 %copy-start.19 = (s32[1,256]{1,0:T(1,128)S(1)}, s32[1,256]{1,0:T(1,128)}, u32[]{:S(2)}) copy-start(s32[1,256]{1,0:T(1,128)} %param.16) | copy-start | bytes 3076
  9.7 12.1 %copy-start.14 = (bf16[1,4,32,16]{2,3,1,0:T(8,128)(2,1)S(1)}, bf16[1,4,32,16]{2,3,1,0:T(8,128)(2,1)}, u32[]{:S(2)}) copy-start(bf16[1,4,32,16]{2,3,1,0:T(8,128)(2,1)} %param.18) | copy-start | bytes 12292
  9.7 12.3 %copy-start.16 = (bf16[4,384]{1,0:T(4,128)(2,1)S(1)}, bf16[4,384]{1,0:T(4,128)(2,1)}, u32[]{:S(2)}) copy-start(bf16[4,384]{1,0:T(4,128)(2,1)} %param.23) | copy-start | bytes 9220
  11.7 22.4 %all-to-all-start = ((bf16[16,2,2,8192]{3,2,1,0:T(2,128)(2,1)}), bf16[16,2,2,8192]{3,2,1,0:T(2,128)(2,1)}, u32[]{:S(2)}, u32[]{:S(2)}) async-start(bf16[16,2,2,8192]{3,2,1,0:T(2,128)(2,1)} %broadcast_select_fusion), calls=%async_computation.1 | async-start | bytes 2097152 | tf_op jit(solution)/shard_map/all_to_all | solution.py:116
  19.0 4.5 %copy-start.7 = (bf16[384,384]{1,0:T(8,128)(2,1)S(1)}, bf16[384,384]{1,0:T(8,128)(2,1)}, u32[]{:S(2)}) copy-start(bf16[384,384]{1,0:T(8,128)(2,1)} %param.22) | copy-start | bytes 884740
  19.0 36.3 %reduce-scatter.2.cloned.1.call-start = ((), (), s32[]{:S(2)}) async-start(), calls=%async_computation.2 | async-start | bytes 73728 | tf_op jit(solution)/shard_map/reduce_scatter | solution.py:102
  21.7 235.8 %all-reduce.7.cloned.1.call-start = ((), (), s32[]{:S(2)}) async-start(), calls=%async_computation.3 | async-start | bytes 5111808 | tf_op jit(solution)/shard_map/psum | solution.py:131
  37.5 20.3 %copy-start.12 = (bf16[128,384]{1,0:T(8,128)(2,1)S(1)}, bf16[128,384]{1,0:T(8,128)(2,1)}, u32[]{:S(2)}) copy-start(bf16[128,384]{1,0:T(8,128)(2,1)} %param.19) | copy-start | bytes 294916
  40.2 18.1 %copy-start.13 = (f32[384]{0:T(512)S(1)}, f32[384]{0:T(512)}, u32[]{:S(2)}) copy-start(f32[384]{0:T(512)} %param.20) | copy-start | bytes 4612
  74.2 2.4 copy-start.6
  76.6 1.9 copy-start.9
  78.5 1.9 copy-start.8
  80.4 2.5 copy-start.2
  82.9 1.7 copy-start.1
  93.4 3.3 copy-start.3
  96.7 1.9 copy-start.4
  101.9 1.2 copy-start.5
  101.9 1.5 copy-start.10
  104.5 244.6 %all-reduce.9.cloned.1.call-start = ((), (), s32[]{:S(2)}) async-start(), calls=%async_computation.4 | async-start | bytes 5111808 | tf_op jit(solution)/shard_map/psum | solution.py:130
  349.1 4.5 %copy-start.11 = (f32[384,384]{1,0:T(8,128)S(1)}, f32[384,384]{1,0:T(8,128)}, u32[]{:S(2)}) copy-start(f32[384,384]{1,0:T(8,128)} %get-tuple-element.33) | copy-start | bytes 1769476
Sparse Core Ops, SparseCore 0:
  22.8 32.3 reduce-scatter.1
  104.6 152.8 all-reduce.6
  260.1 72.9 all-reduce.8
